TPU v7x, 32 devices: a whole 2x2x4 slice. The times are simulated.
32 devices in a mesh: group: 4 (over z), seq: 8 (over y, x, core).
Axes of the slice: x: 2, y: 2, z: 4, core: 2. Of those that a mesh axis runs over, the one named last changes fastest.
Arguments:
- vis_query: bfloat16 [8, 32, 1280], P('group', 'seq'), parts along dimension 0, may hold values from -200 to 200
- vis_key: bfloat16 [8, 32, 1280], P('group', 'seq'), parts along dimension 0, may hold values from -200 to 200
- vis_value: bfloat16 [8, 32, 1280], P('group', 'seq'), parts along dimension 0, may hold values from -6 to 6
- vis_resid: bfloat16 [8, 32, 1280], P('group', 'seq'), parts along dimension 0, may hold values from -6 to 6
- attn_gate: float32 [1], replicated, may hold values from 0.3 to 1.5
- tile_count: int32 [8], P('group'), parts along dimension 0, may hold values from 1 to 4
- w_kv: bfloat16 [1280, 2048], replicated, may hold values from -0.15625 to 0.15625
- text_query: bfloat16 [4096, 6144], P(('group', 'seq')), parts along dimension 0, may hold values from -200 to 200
- text_image: int32 [4096], P(('group', 'seq')), parts along dimension 0, may hold values from 0 to 1, as said below
Outputs:
- vision_out: bfloat16 [8, 32, 1280], P('group', 'seq'), parts along dimension 0
- cross_out: bfloat16 [4096, 6144], P(('group', 'seq')), parts along dimension 0
There are 4 independent parts, one for each index of `group`. A program takes and returns all parts, laid end to end along the dimension named above; an argument that names none is the same for every part. Nothing has to cross between parts.
Inputs may be any that keep to these rules, and one draw needn't show every extreme that they name: `text_image`: does not fall along the sequence; both values occur.
All inputs are finite; a program needn't handle non-finite values.
Results may differ from a plain program's by a relative error of at most 0.0035.
The roundings to bfloat16 on the way count: a program that leaves them out, or rounds other values in their place, can miss the bound.
Values may be sent and summed in bfloat16 or wider, within the bound.
A program may use at most 64 MiB of HBM per device.

v0:
```python
import functools
import math

import jax
import jax.numpy as jnp
from jax import lax
from jax.experimental import pallas as pl
from jax.experimental.pallas import tpu as pltpu
from jax.sharding import PartitionSpec as P

VHEADS = 16
VHEAD = 80
KVH = 8
HD = 128
QGROUP = 6
TILES = 4
LANES = 128
NEG = -1e30


def vision_attend(query, keys, values, tile_count, nheads):
    images, rows, width = query.shape
    length = keys.shape[1]
    patch = length // TILES
    tile_of = jnp.arange(length, dtype=jnp.int32) // patch
    key_ok = tile_of[None, :] < tile_count[:, None]
    query = query.reshape(images, rows, nheads, VHEAD)
    keys = keys.reshape(images, length, nheads, VHEAD)
    values = values.reshape(images, length, nheads, VHEAD)
    scores = jnp.einsum(
        "bqhd,bkhd->bhqk", query, keys, preferred_element_type=jnp.float32
    ) / math.sqrt(VHEAD)
    scores = jnp.where(key_ok[:, None, None, :], scores, NEG)
    peak = jnp.max(scores, axis=-1, keepdims=True)
    expo = jnp.exp(scores - peak)
    probs = (expo / jnp.sum(expo, axis=-1, keepdims=True)).astype(jnp.bfloat16)
    attn = jnp.einsum("bhqk,bkhd->bqhd", probs, values, preferred_element_type=jnp.float32)
    return attn.reshape(images, rows, width)


def general_form(
    vis_query, vis_key, vis_value, vis_resid, attn_gate, tile_count, w_kv, text_query, text_image
):
    images, rows, width = vis_query.shape
    keys, values = (
        lax.all_gather(vis_key, "seq", axis=1, tiled=True),
        lax.all_gather(vis_value, "seq", axis=1, tiled=True),
    )
    attn = vision_attend(vis_query, keys, values, tile_count, VHEADS)
    vision_out = (vis_resid.astype(jnp.float32) + jnp.tanh(attn_gate[0]) * attn).astype(
        jnp.bfloat16
    )
    local_kv = jnp.dot(
        vision_out.reshape(images * rows, width), w_kv, preferred_element_type=jnp.float32
    )
    local_kv = local_kv.astype(jnp.bfloat16).reshape(images, rows, w_kv.shape[1])
    cross_kv = lax.all_gather(local_kv, "seq", axis=1, tiled=True)
    length = cross_kv.shape[1]
    patch = length // TILES
    tile_of = jnp.arange(length, dtype=jnp.int32) // patch
    key_ok = tile_of[None, :] < tile_count[:, None]
    half = KVH * HD
    flat_kv = cross_kv.reshape(images * length, 2 * half)
    cross_key = flat_kv[:, :half].reshape(images * length, KVH, HD)
    cross_value = flat_kv[:, half:].reshape(images * length, KVH, HD)
    image_of_key = jnp.arange(images * length, dtype=jnp.int32) // length
    flat_ok = key_ok.reshape(images * length)
    tokens = text_query.shape[0]
    qrows = text_query.reshape(tokens, KVH, QGROUP, HD)
    score = jnp.einsum(
        "tgqd,kgd->tgqk", qrows, cross_key, preferred_element_type=jnp.float32
    ) / math.sqrt(HD)
    allowed = (image_of_key[None, :] <= text_image[:, None]) & flat_ok[None, :]
    score = jnp.where(allowed[:, None, None, :], score, NEG)
    top = jnp.max(score, axis=-1, keepdims=True)
    expd = jnp.exp(score - top)
    prob = (expd / jnp.sum(expd, axis=-1, keepdims=True)).astype(jnp.bfloat16)
    out = jnp.einsum("tgqk,kgd->tgqd", prob, cross_value, preferred_element_type=jnp.float32)
    cross_out = out.reshape(tokens, KVH * QGROUP * HD).astype(jnp.bfloat16)
    return (vision_out, cross_out)


GRANT = 16 * 1024 * 1024
MESH = pl.DeviceIdType.MESH


def spare_rows(images, rows):
    return -(-images * rows // 16) * 16


def vision_kernel(
    n, images, rows, width, tokens,
    gate_in, count_in, seen_in, q_in, k_in, v_in, r_in, w_in,
    pack_ref,
    slots, stage, w_vmem, vis_all, seen_ref, gate_ref, count_ref,
    load_sem, w_sem, small_sem, send_sem, recv_sem,
):
    me = lax.axis_index("seq")
    chips = n // 2
    half = chips // 2
    chip, core = me // 2, me % 2
    partner = chip * 2 + (1 - core)
    length = n * rows
    keys = images * length
    pair = 2 * rows

    loads = [
        pltpu.make_async_copy(ref.at[b], slots.at[me, b, a], load_sem.at[b, a])
        for b in range(images)
        for a, ref in enumerate((q_in, k_in, v_in, r_in))
    ]
    peers = []
    for ky in range(half):
        for kx in range(2):
            if ky or kx:
                there = ((chip // 2 + ky) % half) * 2 + (chip % 2 + kx) % 2
                peers.append((there, there * 2 + core, there * 2 + (1 - core)))

    barrier = pltpu.get_barrier_semaphore()
    for dev in [dev for _, dev, _ in peers] + [partner]:
        pl.semaphore_signal(barrier, inc=1, device_id={"seq": dev}, device_id_type=MESH)
    for load in loads:
        load.start()
    small = [
        pltpu.make_async_copy(gate_in, gate_ref, small_sem.at[0]),
        pltpu.make_async_copy(count_in, count_ref, small_sem.at[1]),
        pltpu.make_async_copy(seen_in, seen_ref, small_sem.at[2]),
    ]
    for copy in small:
        copy.start()
    w_copy = pltpu.make_async_copy(w_in, w_vmem, w_sem)
    w_copy.start()
    pl.semaphore_wait(barrier, len(peers) + 1)
    for load in loads:
        load.wait()

    def send(slot, b, dev, number):
        return pltpu.make_async_remote_copy(
            src_ref=slots.at[slot, b],
            dst_ref=slots.at[slot, b],
            send_sem=send_sem.at[b, number],
            recv_sem=recv_sem.at[b, slot],
            device_id={"seq": dev},
            device_id_type=MESH,
        )

    sent = []
    for b in range(images):
        for number, (_, dev, _) in reversed(list(enumerate(peers))):
            sent.append(send(me, b, dev, number))
        sent.append(send(me, b, partner, len(peers)))
    for copy in sent:
        copy.start()

    for copy in small:
        copy.wait()
    place = lax.broadcasted_iota(jnp.int32, (length, tokens), 0)
    kv_width = w_vmem.shape[1]
    for b in range(images):
        ok = (place // (length // TILES) < count_ref[b]) & (seen_ref[...] >= b)
        pack_ref[b * length : (b + 1) * length, kv_width : kv_width + tokens] = jnp.where(
            ok, 0.0, NEG
        ).astype(jnp.bfloat16)
    gate = jnp.tanh(jnp.full((1, LANES), gate_ref[0], jnp.float32))

    def arrived(slot, b):
        send(slot, b, partner, 0).wait_recv()

    def forward(b):
        for i, (_, dev, _) in enumerate(peers):
            arrived(dev, b)
            relay = send(dev, b, partner, len(peers) + 1 + i)
            relay.start()
            sent.append(relay)

    def unpack(there, b):
        at = pl.multiple_of(there * pair, pair)
        for a in range(4):
            two = [slots[there * 2 + c, b, a].astype(jnp.float32) for c in range(2)]
            stage[b, a, pl.ds(at, pair), :] = jnp.concatenate(two, axis=0)

    def gather(b):
        arrived(partner, b)
        unpack(chip, b)
        for there, _, other in peers:
            arrived(other, b)
            unpack(there, b)

    heads = width // VHEAD
    side = LANES // length
    key_row = lax.broadcasted_iota(jnp.int32, (length, LANES), 0)
    scale = math.log2(math.e) / math.sqrt(VHEAD)

    def attend(b):
        query = stage[b, 0].astype(jnp.bfloat16)
        key = stage[b, 1].astype(jnp.bfloat16)
        value = stage[b, 2].astype(jnp.bfloat16)
        bias = jnp.where(key_row // (length // TILES) < count_ref[b], 0.0, NEG)
        parts = [None] * (width // LANES)
        for h in range(0, heads, side):
            t0, t1 = h * VHEAD // LANES, -(-(h + side) * VHEAD // LANES)
            lo, hi = t0 * LANES, t1 * LANES
            lane = lax.broadcasted_iota(jnp.int32, (length, hi - lo), 1) + lo
            own = [
                (lane >= i * VHEAD) & (lane < (i + 1) * VHEAD) for i in range(h, h + side)
            ]
            window = query[:, lo:hi]
            spread = jnp.concatenate(
                [jnp.where(mask, window, jnp.zeros_like(window)) for mask in own], axis=0
            )
            score = lax.dot_general(
                key[:, lo:hi], spread, (((1,), (1,)), ((), ())),
                preferred_element_type=jnp.float32,
            )
            score = score + bias
            expo = jnp.exp2((score - jnp.max(score, axis=0, keepdims=True)) * scale)
            prob = expo * (1.0 / jnp.sum(expo, axis=0, keepdims=True))
            attn = lax.dot_general(
                prob.astype(jnp.bfloat16), value[:, lo:hi], (((0,), (0,)), ((), ())),
                preferred_element_type=jnp.float32,
            )
            total = jnp.zeros((length, hi - lo), jnp.float32)
            for i, mask in enumerate(own):
                total = jnp.where(mask, attn[i * length : (i + 1) * length], total)
            for t in range(t0, t1):
                piece = total[:, (t - t0) * LANES : (t - t0 + 1) * LANES]
                parts[t] = piece if parts[t] is None else parts[t] + piece
        for t, part in enumerate(parts):
            cols = slice(t * LANES, (t + 1) * LANES)
            vis_all[b, :, cols] = stage[b, 3, :, cols] + gate * part

    def project(b):
        vis = vis_all[b].astype(jnp.bfloat16)
        step = 2 * LANES
        for j in range(w_vmem.shape[1] // step):
            cols = slice(j * step, (j + 1) * step)
            pack_ref[b * length : (b + 1) * length, cols] = jnp.dot(
                vis, w_vmem[:, cols], preferred_element_type=jnp.float32
            ).astype(jnp.bfloat16)

    forward(0)
    gather(0)
    attend(0)
    w_copy.wait()
    for b in range(1, images):
        forward(b)
        project(b - 1)
        gather(b)
        attend(b)
    project(images - 1)
    mine = []
    for b in range(images):
        near = vis_all[b, pl.ds(pl.multiple_of(chip * pair, pair), pair), :]
        mine.append(jnp.where(core == 0, near[:rows], near[rows:]))
    mine.extend([jnp.zeros_like(mine[0])] * (spare_rows(images, rows) // rows - images))
    pack_ref[keys:, :width] = jnp.concatenate(mine, axis=0).astype(jnp.bfloat16)
    for copy in sent:
        copy.wait_send()


def vision_part(n, q, k, v, r, gate, count, seen, w_kv):
    images, rows, width = q.shape
    length = n * rows
    keys = images * length
    tokens = seen.shape[0]
    anyspace = pl.BlockSpec(memory_space=pltpu.HBM)
    vmem = pl.BlockSpec(memory_space=pltpu.VMEM)
    return pl.pallas_call(
        functools.partial(vision_kernel, n, images, rows, width, tokens),
        out_shape=jax.ShapeDtypeStruct(
            (keys + spare_rows(images, rows), w_kv.shape[1] + tokens), jnp.bfloat16
        ),
        in_specs=[anyspace] * 8,
        out_specs=vmem,
        scratch_shapes=[
            pltpu.VMEM((n, images, 4, rows, width), jnp.bfloat16),
            pltpu.VMEM((images, 4, length, width), jnp.float32),
            pltpu.VMEM(w_kv.shape, jnp.bfloat16),
            pltpu.VMEM((images, length, width), jnp.float32),
            pltpu.VMEM((1, tokens), jnp.int32),
            pltpu.SMEM((1,), jnp.float32),
            pltpu.SMEM((images,), jnp.int32),
            pltpu.SemaphoreType.DMA((images, 4)),
            pltpu.SemaphoreType.DMA,
            pltpu.SemaphoreType.DMA((3,)),
            pltpu.SemaphoreType.DMA((images, n)),
            pltpu.SemaphoreType.DMA((images, n)),
        ],
        compiler_params=pltpu.CompilerParams(
            collective_id=0, has_side_effects=True
        ),
        name="vision",
    )(gate, count, seen.reshape(1, tokens), q, k, v, r, w_kv)


def text_kernel(pack_ref, q_ref, vis_out, out_hbm, o_ref, bias_ref, out_sem):
    images, rows, width = vis_out.shape
    keys, tokens = bias_ref.shape[0] // 2, bias_ref.shape[1]
    for b in range(images):
        vis_out[b] = pack_ref[keys + b * rows : keys + (b + 1) * rows, :width]
    for twin in range(2):
        bias_ref[twin * keys : (twin + 1) * keys, :] = pack_ref[
            :keys, 2 * KVH * HD : 2 * KVH * HD + tokens
        ].astype(jnp.float32)
    scale = math.log2(math.e) / math.sqrt(HD)
    span = QGROUP * HD
    copies = []
    for g in range(KVH):
        k_g = pack_ref[:keys, g * HD : (g + 1) * HD]
        v_g = pack_ref[:keys, (KVH + g) * HD : (KVH + g + 1) * HD]
        zero = jnp.zeros_like(k_g)
        k_two = jnp.concatenate(
            [jnp.concatenate([k_g, zero], axis=1), jnp.concatenate([zero, k_g], axis=1)], axis=0
        )
        v_two = jnp.concatenate(
            [jnp.concatenate([v_g, zero], axis=1), jnp.concatenate([zero, v_g], axis=1)], axis=0
        )
        for j in range(QGROUP // 2):
            cols = slice(g * span + 2 * j * HD, g * span + (2 * j + 2) * HD)
            score = lax.dot_general(
                k_two, q_ref[:, cols], (((1,), (1,)), ((), ())),
                preferred_element_type=jnp.float32,
            )
            score = score + bias_ref[...]
            probs = []
            for part in (score[:keys], score[keys:]):
                expd = jnp.exp2((part - jnp.max(part, axis=0, keepdims=True)) * scale)
                probs.append(expd * (1.0 / jnp.sum(expd, axis=0, keepdims=True)))
            prob = jnp.concatenate(probs, axis=0).astype(jnp.bfloat16)
            o_ref[:, cols] = lax.dot_general(
                prob, v_two, (((0,), (0,)), ((), ())), preferred_element_type=jnp.float32
            ).astype(jnp.bfloat16)
        cols = pl.ds(g * span, span)
        copies.append(
            pltpu.make_async_copy(o_ref.at[:, cols], out_hbm.at[:, cols], out_sem.at[g])
        )
        copies[-1].start()
    for copy in copies:
        copy.wait()


def text_part(shape, keys, pack, query):
    vmem = pl.BlockSpec(memory_space=pltpu.VMEM)
    return pl.pallas_call(
        text_kernel,
        out_shape=(
            jax.ShapeDtypeStruct(shape, jnp.bfloat16),
            jax.ShapeDtypeStruct(query.shape, jnp.bfloat16),
        ),
        in_specs=[vmem] * 2,
        out_specs=(vmem, pl.BlockSpec(memory_space=pl.ANY)),
        scratch_shapes=[
            pltpu.VMEM(query.shape, jnp.bfloat16),
            pltpu.VMEM((2 * keys, query.shape[0]), jnp.float32),
            pltpu.SemaphoreType.DMA((KVH,)),
        ],
        compiler_params=pltpu.CompilerParams(vmem_limit_bytes=GRANT),
        name="text",
    )(pack, query)


def fits(n, images, rows, width):
    length = n * rows
    return (
        n % 4 == 0
        and 2 * images * length == LANES
        and LANES % length == 0
        and (width // VHEAD) % (LANES // length) == 0
        and (2 * rows) % 8 == 0
        and length % 16 == 0
        and spare_rows(images, rows) % rows == 0
    )


def on_device(n, *args):
    vis_query, vis_key, vis_value, vis_resid, attn_gate, tile_count, w_kv, text_query, text_image = args
    images, rows, width = vis_query.shape
    if not fits(n, images, rows, width):
        return general_form(*args)
    pack = vision_part(
        n, vis_query, vis_key, vis_value, vis_resid, attn_gate, tile_count, text_image, w_kv
    )
    return text_part(vis_query.shape, images * rows * n, pack, text_query)


def solution(mesh):
    placed = (
        P("group", "seq", None),
        P("group", "seq", None),
        P("group", "seq", None),
        P("group", "seq", None),
        P(),
        P("group"),
        P(),
        P(("group", "seq"), None),
        P(("group", "seq")),
    )
    return jax.shard_map(
        functools.partial(on_device, mesh.shape["seq"]),
        mesh=mesh,
        in_specs=placed,
        out_specs=(P("group", "seq", None), P(("group", "seq"), None)),
        check_vma=False,
    )
```

profile of v0, /device:TPU:0, one launch (start us, length us, event | category | flops | bytes accessed | tf_op | source)
XLA Modules:
  0.0 19.1 jit_solution(2033016674978517590)
XLA Ops:
  1.3 0.0 copy-start
  1.3 14.1 %vision.1.pack_ref = bf16[80,2176]{1,0:T(8,128)(2,1)} custom-call(f32[1]{0:T(128)S(6)} %copy.11.gate_in, s32[2]{0:T(128)} %count_in.1, s32[1,128]{1,0:T(1,128)} %bitcast.1, bf16[2,4,1280]{2,1,0:T(4,128)(2,1)} %q_in.1, bf16[2,4,1280]{2,1,0:T(4,128)(2,1)} %k_in.1, bf16[2,4,1280]{2,1,0:T(4,128)(2,1)} %v_in.1, bf16[2,4,1280]{2,1,0:T(4,128)(2,1)} %r_in.1, ...), custom_call_target="tpu_custom_call" | custom-call | tf_op jit(solution)/shard_map/vision/pallas_call | solution.py:268
  15.4 0.0 copy-done
  15.4 0.0 copy-start.1
  15.4 1.0 %copy-done.1 = bf16[80,2176]{1,0:T(8,128)(2,1)S(1)} copy-done((bf16[80,2176]{1,0:T(8,128)(2,1)S(1)}, bf16[80,2176]{1,0:T(8,128)(2,1)}, u32[]{:S(2)}) %copy-start.1) | copy-done | bytes 348184
  16.4 2.8 %text.1 = (bf16[2,4,1280]{2,1,0:T(4,128)(2,1)}, bf16[128,6144]{1,0:T(8,128)(2,1)}) custom-call(bf16[80,2176]{1,0:T(8,128)(2,1)S(1)} %copy-done.1, bf16[128,6144]{1,0:T(8,128)(2,1)S(1)} %copy-done), custom_call_target="tpu_custom_call" | custom-call | tf_op jit(solution)/shard_map/text/pallas_call | solution.py:344
Async XLA Ops:
  1.3 14.1 %copy-start = (bf16[128,6144]{1,0:T(8,128)(2,1)S(1)}, bf16[128,6144]{1,0:T(8,128)(2,1)}, u32[]{:S(2)}) copy-start(bf16[128,6144]{1,0:T(8,128)(2,1)} %q_ref.1) | copy-start | bytes 4718596
  15.4 1.0 %copy-start.1 = (bf16[80,2176]{1,0:T(8,128)(2,1)S(1)}, bf16[80,2176]{1,0:T(8,128)(2,1)}, u32[]{:S(2)}) copy-start(bf16[80,2176]{1,0:T(8,128)(2,1)} %vision.1.pack_ref) | copy-start | bytes 1044484
where the time goes:
time: 19.3 us; the launch traced here: 19.1 us
  Pallas kernels  16.9 us (88%)
  between operations  1.31 us (7%)
  local copies, waits for them, and re-layouts  0.98 us (5%)
    pallas_call x1, Pallas kernels, vision_part(): pl.pallas_call(functools.partial(vision_kernel, n, images, rows, width, t...  14.1 us
    pallas_call x1, Pallas kernels, text_part(): pl.pallas_call(text_kernel, out_shape=(jax.ShapeDtypeStruct(shape, jnp.bf...  2.79 us
    unnamed x4, local copies, waits for them, and re-layouts  0.98 us

commit v1 on v0

v1 whole, which is shorter than its diff:
```python
import functools
import math

import jax
import jax.numpy as jnp
from jax import lax
from jax.experimental import pallas as pl
from jax.experimental.pallas import tpu as pltpu
from jax.sharding import PartitionSpec as P

VHEADS = 16
VHEAD = 80
KVH = 8
HD = 128
QGROUP = 6
TILES = 4
LANES = 128
NEG = -1e30


def vision_attend(query, keys, values, tile_count, nheads):
    images, rows, width = query.shape
    length = keys.shape[1]
    patch = length // TILES
    tile_of = jnp.arange(length, dtype=jnp.int32) // patch
    key_ok = tile_of[None, :] < tile_count[:, None]
    query = query.reshape(images, rows, nheads, VHEAD)
    keys = keys.reshape(images, length, nheads, VHEAD)
    values = values.reshape(images, length, nheads, VHEAD)
    scores = jnp.einsum(
        "bqhd,bkhd->bhqk", query, keys, preferred_element_type=jnp.float32
    ) / math.sqrt(VHEAD)
    scores = jnp.where(key_ok[:, None, None, :], scores, NEG)
    peak = jnp.max(scores, axis=-1, keepdims=True)
    expo = jnp.exp(scores - peak)
    probs = (expo / jnp.sum(expo, axis=-1, keepdims=True)).astype(jnp.bfloat16)
    attn = jnp.einsum("bhqk,bkhd->bqhd", probs, values, preferred_element_type=jnp.float32)
    return attn.reshape(images, rows, width)


def general_form(
    vis_query, vis_key, vis_value, vis_resid, attn_gate, tile_count, w_kv, text_query, text_image
):
    images, rows, width = vis_query.shape
    keys, values = (
        lax.all_gather(vis_key, "seq", axis=1, tiled=True),
        lax.all_gather(vis_value, "seq", axis=1, tiled=True),
    )
    attn = vision_attend(vis_query, keys, values, tile_count, VHEADS)
    vision_out = (vis_resid.astype(jnp.float32) + jnp.tanh(attn_gate[0]) * attn).astype(
        jnp.bfloat16
    )
    local_kv = jnp.dot(
        vision_out.reshape(images * rows, width), w_kv, preferred_element_type=jnp.float32
    )
    local_kv = local_kv.astype(jnp.bfloat16).reshape(images, rows, w_kv.shape[1])
    cross_kv = lax.all_gather(local_kv, "seq", axis=1, tiled=True)
    length = cross_kv.shape[1]
    patch = length // TILES
    tile_of = jnp.arange(length, dtype=jnp.int32) // patch
    key_ok = tile_of[None, :] < tile_count[:, None]
    half = KVH * HD
    flat_kv = cross_kv.reshape(images * length, 2 * half)
    cross_key = flat_kv[:, :half].reshape(images * length, KVH, HD)
    cross_value = flat_kv[:, half:].reshape(images * length, KVH, HD)
    image_of_key = jnp.arange(images * length, dtype=jnp.int32) // length
    flat_ok = key_ok.reshape(images * length)
    tokens = text_query.shape[0]
    qrows = text_query.reshape(tokens, KVH, QGROUP, HD)
    score = jnp.einsum(
        "tgqd,kgd->tgqk", qrows, cross_key, preferred_element_type=jnp.float32
    ) / math.sqrt(HD)
    allowed = (image_of_key[None, :] <= text_image[:, None]) & flat_ok[None, :]
    score = jnp.where(allowed[:, None, None, :], score, NEG)
    top = jnp.max(score, axis=-1, keepdims=True)
    expd = jnp.exp(score - top)
    prob = (expd / jnp.sum(expd, axis=-1, keepdims=True)).astype(jnp.bfloat16)
    out = jnp.einsum("tgqk,kgd->tgqd", prob, cross_value, preferred_element_type=jnp.float32)
    cross_out = out.reshape(tokens, KVH * QGROUP * HD).astype(jnp.bfloat16)
    return (vision_out, cross_out)


GRANT = 16 * 1024 * 1024
MESH = pl.DeviceIdType.MESH
CORES = 2


def gather_kernel(
    n, images, rows, width, tokens,
    gate_in, count_in, seen_in, q_in, k_in, v_in, r_in, w_in, text_in,
    vis_ref, bias_ref, pick_ref, w_ref, text_ref,
    own, slots, seen_ref, gate_ref, count_ref,
    load_sem, mine_sem, small_sem, big_sem, send_sem, recv_sem, swap_sem,
):
    me = lax.axis_index("seq")
    chip, core = me // CORES, me % CORES
    row, col = chip // 2, chip % 2
    partner = chip * CORES + (1 - core)
    across = row * 2 + (1 - col)
    along = (1 - row) * 2 + col
    corner = (1 - row) * 2 + (1 - col)
    length = n * rows
    keys = images * length

    sources = (q_in, k_in, v_in, r_in)
    loads = [
        pltpu.make_async_copy(ref.at[b], own.at[b, a], load_sem.at[b, a])
        for b in range(images)
        for a, ref in enumerate(sources)
    ]
    loads += [
        pltpu.make_async_copy(ref.at[core], slots.at[me, a], mine_sem.at[a])
        for a, ref in enumerate(sources)
    ]
    barrier = pltpu.get_barrier_semaphore()
    chips = (corner, across, along)
    others = [there * CORES + b for there in chips for b in range(CORES)] + [partner]
    for dev in others:
        pl.semaphore_signal(barrier, inc=1, device_id={"seq": dev}, device_id_type=MESH)
    for load in loads:
        load.start()
    small = [
        pltpu.make_async_copy(gate_in, gate_ref, small_sem.at[0]),
        pltpu.make_async_copy(count_in, count_ref, small_sem.at[1]),
        pltpu.make_async_copy(seen_in, seen_ref, small_sem.at[2]),
    ]
    big = [
        pltpu.make_async_copy(w_in, w_ref, big_sem.at[0]),
        pltpu.make_async_copy(text_in, text_ref, big_sem.at[1]),
    ]
    for copy in small + big:
        copy.start()
    pl.semaphore_wait(barrier, len(others))
    for load in loads:
        load.wait()

    cuts = (pl.ds(0, 3), pl.ds(3, 1))

    def send(b, part, dev, number):
        return pltpu.make_async_remote_copy(
            src_ref=own.at[b, cuts[part]],
            dst_ref=slots.at[me, cuts[part]],
            send_sem=send_sem.at[part, number],
            recv_sem=recv_sem.at[me, part],
            device_id={"seq": dev},
            device_id_type=MESH,
        )

    sent = []
    for part in range(2):
        for number, there in enumerate(chips):
            for b in range(images):
                sent.append(send(b, part, there * CORES + b, number * CORES + b))
        sent.append(send(1 - core, part, partner, len(chips) * CORES))
    for copy in sent:
        copy.start()

    for copy in small:
        copy.wait()
    place = lax.broadcasted_iota(jnp.int32, (length, tokens), 0)
    for b in range(images):
        ok = (place // (length // TILES) < count_ref[b]) & (seen_ref[...] >= b)
        bias = jnp.where(ok, 0.0, NEG)
        for twin in range(2):
            at = twin * keys + b * length
            bias_ref[at : at + length, :] = bias
    line = lax.broadcasted_iota(jnp.int32, pick_ref.shape, 0)
    want = (line // 8) * length + me * rows + line % 8
    here = lax.broadcasted_iota(jnp.int32, pick_ref.shape, 1)
    pick_ref[...] = jnp.where(here == want, 1.0, 0.0).astype(jnp.bfloat16)
    gate = jnp.tanh(jnp.full((1, LANES), gate_ref[0], jnp.float32))

    def arrived(part):
        for dev in others:
            pltpu.make_async_remote_copy(
                src_ref=own.at[0, cuts[part]],
                dst_ref=slots.at[dev, cuts[part]],
                send_sem=send_sem.at[part, 0],
                recv_sem=recv_sem.at[dev, part],
                device_id={"seq": partner},
                device_id_type=MESH,
            ).wait_recv()

    def whole(a):
        return jnp.concatenate(
            [slots[s, a].astype(jnp.float32) for s in range(n)], axis=0
        )

    arrived(0)
    query, key, value = (whole(a).astype(jnp.bfloat16) for a in range(3))
    heads = width // VHEAD
    side = LANES // length
    groups = range(0, heads, side)
    key_row = lax.broadcasted_iota(jnp.int32, (length, LANES), 0)
    scale = math.log2(math.e) / math.sqrt(VHEAD)
    count = jnp.where(core == 0, count_ref[0], count_ref[1])
    bias = jnp.where(key_row // (length // TILES) < count, 0.0, NEG)
    windows, owners, scores = [], [], []
    for h in groups:
        lo, hi = h * VHEAD // LANES * LANES, -(-(h + side) * VHEAD // LANES) * LANES
        lane = lax.broadcasted_iota(jnp.int32, (length, hi - lo), 1) + lo
        masks = [(lane >= i * VHEAD) & (lane < (i + 1) * VHEAD) for i in range(h, h + side)]
        window = query[:, lo:hi]
        spread = jnp.concatenate(
            [jnp.where(mask, window, jnp.zeros_like(window)) for mask in masks], axis=0
        )
        score = lax.dot_general(
            key[:, lo:hi], spread, (((1,), (1,)), ((), ())),
            preferred_element_type=jnp.float32,
        )
        windows.append((lo, hi))
        owners.append(masks)
        scores.append(score + bias)
    probs = []
    for score in scores:
        expo = jnp.exp2((score - jnp.max(score, axis=0, keepdims=True)) * scale)
        prob = expo * (1.0 / jnp.sum(expo, axis=0, keepdims=True))
        probs.append(prob.astype(jnp.bfloat16))
    parts = [None] * (width // LANES)
    for (lo, hi), masks, prob in zip(windows, owners, probs):
        attn = lax.dot_general(
            prob, value[:, lo:hi], (((0,), (0,)), ((), ())),
            preferred_element_type=jnp.float32,
        )
        total = jnp.zeros((length, hi - lo), jnp.float32)
        for i, mask in enumerate(masks):
            total = jnp.where(mask, attn[i * length : (i + 1) * length], total)
        for t in range(lo // LANES, hi // LANES):
            piece = total[:, t * LANES - lo : (t + 1) * LANES - lo]
            parts[t] = piece if parts[t] is None else parts[t] + piece
    branch = jnp.concatenate(parts, axis=1) * jnp.tile(gate, (1, len(parts)))
    arrived(1)
    mine = pl.ds(pl.multiple_of(core * length, length), length)
    vis_ref[mine, :] = (whole(3) + branch).astype(jnp.bfloat16)

    def swap(at):
        return pltpu.make_async_remote_copy(
            src_ref=vis_ref.at[at],
            dst_ref=vis_ref.at[at],
            send_sem=swap_sem.at[0],
            recv_sem=swap_sem.at[1],
            device_id={"seq": partner},
            device_id_type=MESH,
        )

    swap(mine).start()
    for copy in sent:
        copy.wait_send()
    for copy in big:
        copy.wait()
    swap(mine).wait_send()
    swap(pl.ds(pl.multiple_of((1 - core) * length, length), length)).wait_recv()


def gather_part(n, q, k, v, r, gate, count, seen, w_kv, text):
    images, rows, width = q.shape
    length = n * rows
    keys = images * length
    tokens = seen.shape[0]
    hbm = pl.BlockSpec(memory_space=pltpu.HBM)
    vmem = pl.BlockSpec(memory_space=pltpu.VMEM)
    held = [
        pltpu.with_memory_space_constraint(x, pltpu.HBM)
        for x in (count, seen.reshape(1, tokens), q, k, v, r, w_kv, text)
    ]
    return pl.pallas_call(
        functools.partial(gather_kernel, n, images, rows, width, tokens),
        out_shape=(
            jax.ShapeDtypeStruct((keys, width), jnp.bfloat16),
            jax.ShapeDtypeStruct((2 * keys, tokens), jnp.float32),
            jax.ShapeDtypeStruct((8 * images, keys), jnp.bfloat16),
            jax.ShapeDtypeStruct(w_kv.shape, jnp.bfloat16),
            jax.ShapeDtypeStruct(text.shape, jnp.bfloat16),
        ),
        in_specs=[hbm] * 9,
        out_specs=(vmem,) * 5,
        scratch_shapes=[
            pltpu.VMEM((images, 4, rows, width), jnp.bfloat16),
            pltpu.VMEM((n, 4, rows, width), jnp.bfloat16),
            pltpu.VMEM((1, tokens), jnp.int32),
            pltpu.SMEM((1,), jnp.float32),
            pltpu.SMEM((images,), jnp.int32),
            pltpu.SemaphoreType.DMA((images, 4)),
            pltpu.SemaphoreType.DMA((4,)),
            pltpu.SemaphoreType.DMA((3,)),
            pltpu.SemaphoreType.DMA((2,)),
            pltpu.SemaphoreType.DMA((2, n - 1)),
            pltpu.SemaphoreType.DMA((n, 2)),
            pltpu.SemaphoreType.DMA((2,)),
        ],
        compiler_params=pltpu.CompilerParams(
            collective_id=0, has_side_effects=True, vmem_limit_bytes=GRANT
        ),
        name="vision",
    )(gate, *held)


def text_kernel(
    vis_ref, bias_ref, pick_ref, w_ref, q_ref,
    vis_out, out_hbm,
    local_ref, kv_ref, o_ref, local_sem, out_sem,
):
    images, rows, width = local_ref.shape
    keys = vis_ref.shape[0]
    vis = vis_ref[...]
    half = KVH * HD
    scale = math.log2(math.e) / math.sqrt(HD)
    span = QGROUP * HD
    copies = []

    def project(at):
        return jnp.dot(
            vis, w_ref[:, at : at + 2 * HD], preferred_element_type=jnp.float32
        ).astype(jnp.bfloat16)

    def double(x):
        zero = jnp.zeros_like(x)
        return jnp.concatenate(
            [jnp.concatenate([x, zero], axis=1), jnp.concatenate([zero, x], axis=1)], axis=0
        )

    def attend(g, k_two, v_two):
        for j in range(QGROUP // 2):
            cols = slice(g * span + 2 * j * HD, g * span + (2 * j + 2) * HD)
            score = lax.dot_general(
                k_two, q_ref[:, cols], (((1,), (1,)), ((), ())),
                preferred_element_type=jnp.float32,
            )
            score = score + bias_ref[...]
            probs = []
            for part in (score[:keys], score[keys:]):
                expd = jnp.exp2((part - jnp.max(part, axis=0, keepdims=True)) * scale)
                probs.append(expd * (1.0 / jnp.sum(expd, axis=0, keepdims=True)))
            prob = jnp.concatenate(probs, axis=0).astype(jnp.bfloat16)
            o_ref[:, cols] = lax.dot_general(
                prob, v_two, (((0,), (0,)), ((), ())), preferred_element_type=jnp.float32
            ).astype(jnp.bfloat16)
        cols = pl.ds(g * span, span)
        copies.append(
            pltpu.make_async_copy(o_ref.at[:, cols], out_hbm.at[:, cols], out_sem.at[g])
        )
        copies[-1].start()

    local = jnp.dot(pick_ref[...], vis, preferred_element_type=jnp.float32)
    for b in range(images):
        local_ref[b] = local[8 * b : 8 * b + rows].astype(jnp.bfloat16)
    copies.append(pltpu.make_async_copy(local_ref, vis_out, local_sem))
    copies[-1].start()
    for at in range(0, 2 * half, 2 * HD):
        kv_ref[:, at : at + 2 * HD] = project(at)
    for g in range(KVH):
        attend(
            g,
            double(kv_ref[:, g * HD : (g + 1) * HD]),
            double(kv_ref[:, half + g * HD : half + (g + 1) * HD]),
        )
    for copy in copies:
        copy.wait()


def text_part(shape, vis, bias, pick, w_kv, query):
    vmem = pl.BlockSpec(memory_space=pltpu.VMEM)
    anyspace = pl.BlockSpec(memory_space=pl.ANY)
    return pl.pallas_call(
        text_kernel,
        out_shape=(
            jax.ShapeDtypeStruct(shape, jnp.bfloat16),
            jax.ShapeDtypeStruct(query.shape, jnp.bfloat16),
        ),
        in_specs=[vmem] * 5,
        out_specs=(anyspace, anyspace),
        scratch_shapes=[
            pltpu.VMEM(shape, jnp.bfloat16),
            pltpu.VMEM((vis.shape[0], w_kv.shape[1]), jnp.bfloat16),
            pltpu.VMEM(query.shape, jnp.bfloat16),
            pltpu.SemaphoreType.DMA,
            pltpu.SemaphoreType.DMA((KVH,)),
        ],
        compiler_params=pltpu.CompilerParams(vmem_limit_bytes=GRANT),
        name="text",
    )(vis, bias, pick, w_kv, query)


def fits(n, images, rows, width):
    length = n * rows
    return (
        n == 4 * CORES
        and images == CORES
        and 2 * images * length == LANES
        and LANES % length == 0
        and (width // VHEAD) % (LANES // length) == 0
        and rows <= 8
        and length % 16 == 0
    )


def on_device(n, *args):
    vis_query, vis_key, vis_value, vis_resid, attn_gate, tile_count, w_kv, text_query, text_image = args
    images, rows, width = vis_query.shape
    if not fits(n, images, rows, width):
        return general_form(*args)
    held = gather_part(
        n, vis_query, vis_key, vis_value, vis_resid, attn_gate, tile_count, text_image,
        w_kv, text_query,
    )
    return text_part(vis_query.shape, *held)


def solution(mesh):
    placed = (
        P("group", "seq", None),
        P("group", "seq", None),
        P("group", "seq", None),
        P("group", "seq", None),
        P(),
        P("group"),
        P(),
        P(("group", "seq"), None),
        P(("group", "seq")),
    )
    return jax.shard_map(
        functools.partial(on_device, mesh.shape["seq"]),
        mesh=mesh,
        in_specs=placed,
        out_specs=(P("group", "seq", None), P(("group", "seq"), None)),
        check_vma=False,
    )
```

time: 19.3 us -> 16.4 us (0.85)
  Pallas kernels: 16.9 us -> 15 us
  local copies, waits for them, and re-layouts: 0.98 us -> 0 us
    pallas_call x1, Pallas kernels: 14.1 us -> 11.9 us  [gather_part(): pl.pallas_call(functools.partial(gather_kernel, n, images, rows, width, t...]
    unnamed x4 -> x0, local copies, waits for them, and re-layouts: 0.98 us -> none
    pallas_call x1, Pallas kernels: 2.79 us -> 3.09 us  [text_part(): pl.pallas_call(text_kernel, out_shape=(jax.ShapeDtypeStruct(shape, jnp.bf...]
where the time goes in v1:
time: 16.4 us; the launch traced here: 16.3 us
  Pallas kernels  15 us (91%)
  between operations  1.29 us (8%)
    pallas_call x1, Pallas kernels, gather_part(): pl.pallas_call(functools.partial(gather_kernel, n, images, rows, width, t...  11.9 us
    pallas_call x1, Pallas kernels, text_part(): pl.pallas_call(text_kernel, out_shape=(jax.ShapeDtypeStruct(shape, jnp.bf...  3.09 us

profile of v1, /device:TPU:0, one launch (start us, length us, event | category | flops | bytes accessed | tf_op | source)
XLA Modules:
  0.0 16.3 jit_solution(17837774606058577005)
XLA Ops:
  1.3 11.9 %vision.1 = (bf16[64,1280]{1,0:T(8,128)(2,1)S(1)}, f32[128,128]{1,0:T(8,128)S(1)}, bf16[16,64]{1,0:T(8,128)(2,1)S(1)}, bf16[1280,2048]{1,0:T(8,128)(2,1)S(1)}, bf16[128,6144]{1,0:T(8,128)(2,1)S(1)}) custom-call(f32[1]{0:T(128)S(6)} %copy.11.gate_in, s32[2]{0:T(128)} %count_in.1, s32[1,128]{1,0:T(1,128)} %bitcast.1, bf16[2,4,1280]{2,1,0:T(4,128)(2,1)} %q_in.1, ...), custom_call_target="tpu_custom_call" | custom-call | tf_op jit(solution)/shard_map/vision/pallas_call | solution.py:266
  13.2 3.1 %text.1 = (bf16[2,4,1280]{2,1,0:T(4,128)(2,1)}, bf16[128,6144]{1,0:T(8,128)(2,1)}) custom-call(bf16[64,1280]{1,0:T(8,128)(2,1)S(1)} %get-tuple-element.7.vis_ref, f32[128,128]{1,0:T(8,128)S(1)} %get-tuple-element.8.bias_ref, bf16[16,64]{1,0:T(8,128)(2,1)S(1)} %get-tuple-element.9.pick_ref, bf16[1280,2048]{1,0:T(8,128)(2,1)S(1)} %get-tuple-element.10.w_ref, ...), custom_call_target="tpu_custom_call" | custom-call | tf_op jit(solution)/shard_map/text/pallas_call | solution.py:364

commit v2 on v1

--- a/solution.py
+++ b/solution.py
@@ -89,8 +89,8 @@
     n, images, rows, width, tokens,
     gate_in, count_in, seen_in, q_in, k_in, v_in, r_in, w_in, text_in,
     vis_ref, bias_ref, pick_ref, w_ref, text_ref,
-    own, slots, seen_ref, gate_ref, count_ref,
-    load_sem, mine_sem, small_sem, big_sem, send_sem, recv_sem, swap_sem,
+    other, slots, seen_ref, gate_ref, count_ref,
+    load_sem, small_sem, big_sem, send_sem, recv_sem, swap_sem,
 ):
     me = lax.axis_index("seq")
     chip, core = me // CORES, me % CORES
@@ -103,15 +103,16 @@
     keys = images * length
 
     sources = (q_in, k_in, v_in, r_in)
+    mine = slots.at[me]
     loads = [
-        pltpu.make_async_copy(ref.at[b], own.at[b, a], load_sem.at[b, a])
-        for b in range(images)
+        pltpu.make_async_copy(ref.at[image], into.at[a], load_sem)
         for a, ref in enumerate(sources)
+        for image, into in ((core, mine), (1 - core, other))
     ]
-    loads += [
-        pltpu.make_async_copy(ref.at[core], slots.at[me, a], mine_sem.at[a])
-        for a, ref in enumerate(sources)
-    ]
+
+    def all_of(ref, sem):
+        return pltpu.make_async_copy(ref, ref, sem)
+
     barrier = pltpu.get_barrier_semaphore()
     chips = (corner, across, along)
     others = [there * CORES + b for there in chips for b in range(CORES)] + [partner]
@@ -128,31 +129,29 @@
         pltpu.make_async_copy(w_in, w_ref, big_sem.at[0]),
         pltpu.make_async_copy(text_in, text_ref, big_sem.at[1]),
     ]
-    for copy in small + big:
+    for copy in small:
         copy.start()
     pl.semaphore_wait(barrier, len(others))
-    for load in loads:
-        load.wait()
+    all_of(slots.at[:2], load_sem).wait()
 
     cuts = (pl.ds(0, 3), pl.ds(3, 1))
 
-    def send(b, part, dev, number):
-        return pltpu.make_async_remote_copy(
-            src_ref=own.at[b, cuts[part]],
+    def send(src, part, dev):
+        pltpu.make_async_remote_copy(
+            src_ref=src.at[cuts[part]],
             dst_ref=slots.at[me, cuts[part]],
-            send_sem=send_sem.at[part, number],
-            recv_sem=recv_sem.at[me, part],
+            send_sem=send_sem,
+            recv_sem=recv_sem.at[part],
             device_id={"seq": dev},
             device_id_type=MESH,
-        )
-
-    sent = []
+        ).start()
+
     for part in range(2):
-        for number, there in enumerate(chips):
-            for b in range(images):
-                sent.append(send(b, part, there * CORES + b, number * CORES + b))
-        sent.append(send(1 - core, part, partner, len(chips) * CORES))
-    for copy in sent:
+        for there in chips:
+            send(mine, part, there * CORES + core)
+            send(other, part, there * CORES + 1 - core)
+        send(other, part, partner)
+    for copy in big:
         copy.start()
 
     for copy in small:
@@ -166,20 +165,12 @@
             bias_ref[at : at + length, :] = bias
     line = lax.broadcasted_iota(jnp.int32, pick_ref.shape, 0)
     want = (line // 8) * length + me * rows + line % 8
-    here = lax.broadcasted_iota(jnp.int32, pick_ref.shape, 1)
-    pick_ref[...] = jnp.where(here == want, 1.0, 0.0).astype(jnp.bfloat16)
+    key_at = lax.broadcasted_iota(jnp.int32, pick_ref.shape, 1)
+    pick_ref[...] = jnp.where(key_at == want, 1.0, 0.0).astype(jnp.bfloat16)
     gate = jnp.tanh(jnp.full((1, LANES), gate_ref[0], jnp.float32))
 
     def arrived(part):
-        for dev in others:
-            pltpu.make_async_remote_copy(
-                src_ref=own.at[0, cuts[part]],
-                dst_ref=slots.at[dev, cuts[part]],
-                send_sem=send_sem.at[part, 0],
-                recv_sem=recv_sem.at[dev, part],
-                device_id={"seq": partner},
-                device_id_type=MESH,
-            ).wait_recv()
+        all_of(slots.at[: n - 1, cuts[part]], recv_sem.at[part]).wait()
 
     def whole(a):
         return jnp.concatenate(
@@ -230,8 +221,8 @@
             parts[t] = piece if parts[t] is None else parts[t] + piece
     branch = jnp.concatenate(parts, axis=1) * jnp.tile(gate, (1, len(parts)))
     arrived(1)
-    mine = pl.ds(pl.multiple_of(core * length, length), length)
-    vis_ref[mine, :] = (whole(3) + branch).astype(jnp.bfloat16)
+    here = pl.ds(pl.multiple_of(core * length, length), length)
+    vis_ref[here, :] = (whole(3) + branch).astype(jnp.bfloat16)
 
     def swap(at):
         return pltpu.make_async_remote_copy(
@@ -243,12 +234,11 @@
             device_id_type=MESH,
         )
 
-    swap(mine).start()
-    for copy in sent:
-        copy.wait_send()
+    swap(here).start()
+    all_of(slots.at[: n - 1], send_sem).wait()
     for copy in big:
         copy.wait()
-    swap(mine).wait_send()
+    swap(here).wait_send()
     swap(pl.ds(pl.multiple_of((1 - core) * length, length), length)).wait_recv()
 
 
@@ -275,17 +265,16 @@
         in_specs=[hbm] * 9,
         out_specs=(vmem,) * 5,
         scratch_shapes=[
-            pltpu.VMEM((images, 4, rows, width), jnp.bfloat16),
+            pltpu.VMEM((4, rows, width), jnp.bfloat16),
             pltpu.VMEM((n, 4, rows, width), jnp.bfloat16),
             pltpu.VMEM((1, tokens), jnp.int32),
             pltpu.SMEM((1,), jnp.float32),
             pltpu.SMEM((images,), jnp.int32),
-            pltpu.SemaphoreType.DMA((images, 4)),
-            pltpu.SemaphoreType.DMA((4,)),
+            pltpu.SemaphoreType.DMA,
             pltpu.SemaphoreType.DMA((3,)),
             pltpu.SemaphoreType.DMA((2,)),
-            pltpu.SemaphoreType.DMA((2, n - 1)),
-            pltpu.SemaphoreType.DMA((n, 2)),
+            pltpu.SemaphoreType.DMA,
+            pltpu.SemaphoreType.DMA((2,)),
             pltpu.SemaphoreType.DMA((2,)),
         ],
         compiler_params=pltpu.CompilerParams(

time: 16.4 us -> 14.6 us (0.89)
  Pallas kernels: 15 us -> 13.2 us
    pallas_call x1, Pallas kernels: 11.9 us -> 10.1 us  [gather_part(): pl.pallas_call(functools.partial(gather_kernel, n, images, rows, width, t...]
where the time goes in v2:
time: 14.6 us; the launch traced here: 14.5 us
  Pallas kernels  13.2 us (90%)
  between operations  1.29 us (9%)
    pallas_call x1, Pallas kernels, gather_part(): pl.pallas_call(functools.partial(gather_kernel, n, images, rows, width, t...  10.1 us
    pallas_call x1, Pallas kernels, text_part(): pl.pallas_call(text_kernel, out_shape=(jax.ShapeDtypeStruct(shape, jnp.bf...  3.09 us

profile of v2, /device:TPU:0, one launch (start us, length us, event | category | flops | bytes accessed | tf_op | source)
XLA Modules:
  0.0 14.5 jit_solution(16938222518484697305)
XLA Ops:
  1.3 10.1 %vision.1 = (bf16[64,1280]{1,0:T(8,128)(2,1)S(1)}, f32[128,128]{1,0:T(8,128)S(1)}, bf16[16,64]{1,0:T(8,128)(2,1)S(1)}, bf16[1280,2048]{1,0:T(8,128)(2,1)S(1)}, bf16[128,6144]{1,0:T(8,128)(2,1)S(1)}) custom-call(f32[1]{0:T(128)S(6)} %copy.11.gate_in, s32[2]{0:T(128)} %count_in.1, s32[1,128]{1,0:T(1,128)} %bitcast.1, bf16[2,4,1280]{2,1,0:T(4,128)(2,1)} %q_in.1, ...), custom_call_target="tpu_custom_call" | custom-call | tf_op jit(solution)/shard_map/vision/pallas_call | solution.py:256
  11.4 3.1 %text.1 = (bf16[2,4,1280]{2,1,0:T(4,128)(2,1)}, bf16[128,6144]{1,0:T(8,128)(2,1)}) custom-call(bf16[64,1280]{1,0:T(8,128)(2,1)S(1)} %get-tuple-element.7.vis_ref, f32[128,128]{1,0:T(8,128)S(1)} %get-tuple-element.8.bias_ref, bf16[16,64]{1,0:T(8,128)(2,1)S(1)} %get-tuple-element.9.pick_ref, bf16[1280,2048]{1,0:T(8,128)(2,1)S(1)} %get-tuple-element.10.w_ref, ...), custom_call_target="tpu_custom_call" | custom-call | tf_op jit(solution)/shard_map/text/pallas_call | solution.py:353

commit v3 on v2

--- a/solution.py
+++ b/solution.py
@@ -295,7 +295,6 @@
     half = KVH * HD
     scale = math.log2(math.e) / math.sqrt(HD)
     span = QGROUP * HD
-    copies = []
 
     def project(at):
         return jnp.dot(
@@ -309,32 +308,41 @@
         )
 
     def attend(g, k_two, v_two):
-        for j in range(QGROUP // 2):
-            cols = slice(g * span + 2 * j * HD, g * span + (2 * j + 2) * HD)
-            score = lax.dot_general(
-                k_two, q_ref[:, cols], (((1,), (1,)), ((), ())),
-                preferred_element_type=jnp.float32,
+        pairs = QGROUP // 2
+        wide = 2 * HD
+        scores = [
+            lax.dot_general(
+                k_two, q_ref[:, g * span + j * wide : g * span + (j + 1) * wide],
+                (((1,), (1,)), ((), ())), preferred_element_type=jnp.float32,
             )
-            score = score + bias_ref[...]
-            probs = []
+            for j in range(pairs)
+        ]
+        bias = bias_ref[:keys, :]
+        probs = []
+        for score in scores:
+            halves = []
             for part in (score[:keys], score[keys:]):
+                part = part + bias
                 expd = jnp.exp2((part - jnp.max(part, axis=0, keepdims=True)) * scale)
-                probs.append(expd * (1.0 / jnp.sum(expd, axis=0, keepdims=True)))
-            prob = jnp.concatenate(probs, axis=0).astype(jnp.bfloat16)
-            o_ref[:, cols] = lax.dot_general(
-                prob, v_two, (((0,), (0,)), ((), ())), preferred_element_type=jnp.float32
-            ).astype(jnp.bfloat16)
+                halves.append(expd * (1.0 / jnp.sum(expd, axis=0, keepdims=True)))
+            probs.append(jnp.concatenate(halves, axis=0).astype(jnp.bfloat16))
+        out = lax.dot_general(
+            jnp.concatenate(probs, axis=1), v_two, (((0,), (0,)), ((), ())),
+            preferred_element_type=jnp.float32,
+        ).astype(jnp.bfloat16)
+        tokens = out.shape[0] // pairs
+        for j in range(pairs):
+            o_ref[:, g * span + j * wide : g * span + (j + 1) * wide] = out[
+                j * tokens : (j + 1) * tokens
+            ]
         cols = pl.ds(g * span, span)
-        copies.append(
-            pltpu.make_async_copy(o_ref.at[:, cols], out_hbm.at[:, cols], out_sem.at[g])
-        )
-        copies[-1].start()
+        pltpu.make_async_copy(o_ref.at[:, cols], out_hbm.at[:, cols], out_sem).start()
 
     local = jnp.dot(pick_ref[...], vis, preferred_element_type=jnp.float32)
     for b in range(images):
         local_ref[b] = local[8 * b : 8 * b + rows].astype(jnp.bfloat16)
-    copies.append(pltpu.make_async_copy(local_ref, vis_out, local_sem))
-    copies[-1].start()
+    local_copy = pltpu.make_async_copy(local_ref, vis_out, local_sem)
+    local_copy.start()
     for at in range(0, 2 * half, 2 * HD):
         kv_ref[:, at : at + 2 * HD] = project(at)
     for g in range(KVH):
@@ -343,8 +351,8 @@
             double(kv_ref[:, g * HD : (g + 1) * HD]),
             double(kv_ref[:, half + g * HD : half + (g + 1) * HD]),
         )
-    for copy in copies:
-        copy.wait()
+    local_copy.wait()
+    pltpu.make_async_copy(o_ref, out_hbm, out_sem).wait()
 
 
 def text_part(shape, vis, bias, pick, w_kv, query):
@@ -363,7 +371,7 @@
             pltpu.VMEM((vis.shape[0], w_kv.shape[1]), jnp.bfloat16),
             pltpu.VMEM(query.shape, jnp.bfloat16),
             pltpu.SemaphoreType.DMA,
-            pltpu.SemaphoreType.DMA((KVH,)),
+            pltpu.SemaphoreType.DMA,
         ],
         compiler_params=pltpu.CompilerParams(vmem_limit_bytes=GRANT),
         name="text",

time: 14.6 us -> 14.3 us (0.979)
  Pallas kernels: 13.2 us -> 12.9 us
    pallas_call x1, Pallas kernels: 3.09 us -> 2.8 us  [text_part(): pl.pallas_call(text_kernel, out_shape=(jax.ShapeDtypeStruct(shape, jnp.bf...]
where the time goes in v3:
time: 14.3 us; the launch traced here: 14.2 us
  Pallas kernels  12.9 us (90%)
  between operations  1.29 us (9%)
    pallas_call x1, Pallas kernels, gather_part(): pl.pallas_call(functools.partial(gather_kernel, n, images, rows, width, t...  10.1 us
    pallas_call x1, Pallas kernels, text_part(): pl.pallas_call(text_kernel, out_shape=(jax.ShapeDtypeStruct(shape, jnp.bf...  2.8 us

profile of v3, /device:TPU:0, one launch (start us, length us, event | category | flops | bytes accessed | tf_op | source)
XLA Modules:
  0.0 14.2 jit_solution(17981588709225782465)
XLA Ops:
  1.3 10.1 %vision.1 = (bf16[64,1280]{1,0:T(8,128)(2,1)S(1)}, f32[128,128]{1,0:T(8,128)S(1)}, bf16[16,64]{1,0:T(8,128)(2,1)S(1)}, bf16[1280,2048]{1,0:T(8,128)(2,1)S(1)}, bf16[128,6144]{1,0:T(8,128)(2,1)S(1)}) custom-call(f32[1]{0:T(128)S(6)} %copy.11.gate_in, s32[2]{0:T(128)} %count_in.1, s32[1,128]{1,0:T(1,128)} %bitcast.1, bf16[2,4,1280]{2,1,0:T(4,128)(2,1)} %q_in.1, ...), custom_call_target="tpu_custom_call" | custom-call | tf_op jit(solution)/shard_map/vision/pallas_call | solution.py:256
  11.4 2.8 %text.1 = (bf16[2,4,1280]{2,1,0:T(4,128)(2,1)}, bf16[128,6144]{1,0:T(8,128)(2,1)}) custom-call(bf16[64,1280]{1,0:T(8,128)(2,1)S(1)} %get-tuple-element.7.vis_ref, f32[128,128]{1,0:T(8,128)S(1)} %get-tuple-element.8.bias_ref, bf16[16,64]{1,0:T(8,128)(2,1)S(1)} %get-tuple-element.9.pick_ref, bf16[1280,2048]{1,0:T(8,128)(2,1)S(1)} %get-tuple-element.10.w_ref, ...), custom_call_target="tpu_custom_call" | custom-call | tf_op jit(solution)/shard_map/text/pallas_call | solution.py:361

commit v4 on v3

--- a/solution.py
+++ b/solution.py
@@ -88,8 +88,8 @@
 def gather_kernel(
     n, images, rows, width, tokens,
     gate_in, count_in, seen_in, q_in, k_in, v_in, r_in, w_in, text_in,
-    vis_ref, bias_ref, pick_ref, w_ref, text_ref,
-    other, slots, seen_ref, gate_ref, count_ref,
+    vis_ref, bias_ref, pick_ref, kv_ref, text_ref,
+    w_ref, other, slots, seen_ref, gate_ref, count_ref,
     load_sem, small_sem, big_sem, send_sem, recv_sem, swap_sem,
 ):
     me = lax.axis_index("seq")
@@ -224,22 +224,41 @@
     here = pl.ds(pl.multiple_of(core * length, length), length)
     vis_ref[here, :] = (whole(3) + branch).astype(jnp.bfloat16)
 
-    def swap(at):
+    there = pl.ds(pl.multiple_of((1 - core) * length, length), length)
+    half = KVH * HD
+
+    def swap(ref, at, number):
         return pltpu.make_async_remote_copy(
-            src_ref=vis_ref.at[at],
-            dst_ref=vis_ref.at[at],
-            send_sem=swap_sem.at[0],
-            recv_sem=swap_sem.at[1],
+            src_ref=ref.at[at],
+            dst_ref=ref.at[at],
+            send_sem=swap_sem.at[number],
+            recv_sem=swap_sem.at[number + 1],
             device_id={"seq": partner},
             device_id_type=MESH,
         )
 
-    swap(here).start()
-    all_of(slots.at[: n - 1], send_sem).wait()
+    def project(at, first, last):
+        vis = vis_ref[at, :]
+        for start in range(first, last, 2 * HD):
+            cols = slice(start, start + 2 * HD)
+            kv_ref[at, cols] = jnp.dot(
+                vis, w_ref[:, cols], preferred_element_type=jnp.float32
+            ).astype(jnp.bfloat16)
+
+    vis_swap = swap(vis_ref, here, 0)
+    key_swap = swap(kv_ref, (here, pl.ds(0, half)), 2)
+    vis_swap.start()
     for copy in big:
         copy.wait()
-    swap(here).wait_send()
-    swap(pl.ds(pl.multiple_of((1 - core) * length, length), length)).wait_recv()
+    project(here, 0, half)
+    key_swap.start()
+    project(here, half, 2 * half)
+    swap(vis_ref, there, 0).wait_recv()
+    project(there, half, 2 * half)
+    all_of(slots.at[: n - 1], send_sem).wait()
+    vis_swap.wait_send()
+    key_swap.wait_send()
+    swap(kv_ref, (there, pl.ds(0, half)), 2).wait_recv()
 
 
 def gather_part(n, q, k, v, r, gate, count, seen, w_kv, text):
@@ -259,12 +278,13 @@
             jax.ShapeDtypeStruct((keys, width), jnp.bfloat16),
             jax.ShapeDtypeStruct((2 * keys, tokens), jnp.float32),
             jax.ShapeDtypeStruct((8 * images, keys), jnp.bfloat16),
-            jax.ShapeDtypeStruct(w_kv.shape, jnp.bfloat16),
+            jax.ShapeDtypeStruct((keys, w_kv.shape[1]), jnp.bfloat16),
             jax.ShapeDtypeStruct(text.shape, jnp.bfloat16),
         ),
         in_specs=[hbm] * 9,
         out_specs=(vmem,) * 5,
         scratch_shapes=[
+            pltpu.VMEM(w_kv.shape, jnp.bfloat16),
             pltpu.VMEM((4, rows, width), jnp.bfloat16),
             pltpu.VMEM((n, 4, rows, width), jnp.bfloat16),
             pltpu.VMEM((1, tokens), jnp.int32),
@@ -275,7 +295,7 @@
             pltpu.SemaphoreType.DMA((2,)),
             pltpu.SemaphoreType.DMA,
             pltpu.SemaphoreType.DMA((2,)),
-            pltpu.SemaphoreType.DMA((2,)),
+            pltpu.SemaphoreType.DMA((4,)),
         ],
         compiler_params=pltpu.CompilerParams(
             collective_id=0, has_side_effects=True, vmem_limit_bytes=GRANT
@@ -285,21 +305,15 @@
 
 
 def text_kernel(
-    vis_ref, bias_ref, pick_ref, w_ref, q_ref,
+    vis_ref, bias_ref, pick_ref, kv_ref, q_ref,
     vis_out, out_hbm,
-    local_ref, kv_ref, o_ref, local_sem, out_sem,
+    local_ref, o_ref, local_sem, out_sem,
 ):
     images, rows, width = local_ref.shape
     keys = vis_ref.shape[0]
-    vis = vis_ref[...]
     half = KVH * HD
     scale = math.log2(math.e) / math.sqrt(HD)
     span = QGROUP * HD
-
-    def project(at):
-        return jnp.dot(
-            vis, w_ref[:, at : at + 2 * HD], preferred_element_type=jnp.float32
-        ).astype(jnp.bfloat16)
 
     def double(x):
         zero = jnp.zeros_like(x)
@@ -338,13 +352,11 @@
         cols = pl.ds(g * span, span)
         pltpu.make_async_copy(o_ref.at[:, cols], out_hbm.at[:, cols], out_sem).start()
 
-    local = jnp.dot(pick_ref[...], vis, preferred_element_type=jnp.float32)
+    local = jnp.dot(pick_ref[...], vis_ref[...], preferred_element_type=jnp.float32)
     for b in range(images):
         local_ref[b] = local[8 * b : 8 * b + rows].astype(jnp.bfloat16)
     local_copy = pltpu.make_async_copy(local_ref, vis_out, local_sem)
     local_copy.start()
-    for at in range(0, 2 * half, 2 * HD):
-        kv_ref[:, at : at + 2 * HD] = project(at)
     for g in range(KVH):
         attend(
             g,
@@ -355,7 +367,7 @@
     pltpu.make_async_copy(o_ref, out_hbm, out_sem).wait()
 
 
-def text_part(shape, vis, bias, pick, w_kv, query):
+def text_part(shape, vis, bias, pick, kv, query):
     vmem = pl.BlockSpec(memory_space=pltpu.VMEM)
     anyspace = pl.BlockSpec(memory_space=pl.ANY)
     return pl.pallas_call(
@@ -368,14 +380,13 @@
         out_specs=(anyspace, anyspace),
         scratch_shapes=[
             pltpu.VMEM(shape, jnp.bfloat16),
-            pltpu.VMEM((vis.shape[0], w_kv.shape[1]), jnp.bfloat16),
             pltpu.VMEM(query.shape, jnp.bfloat16),
             pltpu.SemaphoreType.DMA,
             pltpu.SemaphoreType.DMA,
         ],
         compiler_params=pltpu.CompilerParams(vmem_limit_bytes=GRANT),
         name="text",
-    )(vis, bias, pick, w_kv, query)
+    )(vis, bias, pick, kv, query)
 
 
 def fits(n, images, rows, width):

time: 14.3 us -> 14.1 us (0.986)
  Pallas kernels: 12.9 us -> 12.7 us
    pallas_call x1, Pallas kernels: 2.8 us -> 1.93 us  [text_part(): pl.pallas_call(text_kernel, out_shape=(jax.ShapeDtypeStruct(shape, jnp.bf...]
    pallas_call x1, Pallas kernels: 10.1 us -> 10.8 us  [gather_part(): pl.pallas_call(functools.partial(gather_kernel, n, images, rows, width, t...]
where the time goes in v4:
time: 14.1 us; the launch traced here: 14 us
  Pallas kernels  12.7 us (90%)
  between operations  1.29 us (9%)
    pallas_call x1, Pallas kernels, gather_part(): pl.pallas_call(functools.partial(gather_kernel, n, images, rows, width, t...  10.8 us
    pallas_call x1, Pallas kernels, text_part(): pl.pallas_call(text_kernel, out_shape=(jax.ShapeDtypeStruct(shape, jnp.bf...  1.93 us

profile of v4, /device:TPU:0, one launch (start us, length us, event | category | flops | bytes accessed | tf_op | source)
XLA Modules:
  0.0 14.0 jit_solution(12934801933681971624)
XLA Ops:
  1.3 10.8 %vision.1 = (bf16[64,1280]{1,0:T(8,128)(2,1)S(1)}, f32[128,128]{1,0:T(8,128)S(1)}, bf16[16,64]{1,0:T(8,128)(2,1)S(1)}, bf16[64,2048]{1,0:T(8,128)(2,1)S(1)}, bf16[128,6144]{1,0:T(8,128)(2,1)S(1)}) custom-call(f32[1]{0:T(128)S(6)} %copy.11.gate_in, s32[2]{0:T(128)} %count_in.1, s32[1,128]{1,0:T(1,128)} %bitcast.1, bf16[2,4,1280]{2,1,0:T(4,128)(2,1)} %q_in.1, ...), custom_call_target="tpu_custom_call" | custom-call | tf_op jit(solution)/shard_map/vision/pallas_call | solution.py:275
  12.0 1.9 %text.1 = (bf16[2,4,1280]{2,1,0:T(4,128)(2,1)}, bf16[128,6144]{1,0:T(8,128)(2,1)}) custom-call(bf16[64,1280]{1,0:T(8,128)(2,1)S(1)} %get-tuple-element.7.vis_ref, f32[128,128]{1,0:T(8,128)S(1)} %get-tuple-element.8.bias_ref, bf16[16,64]{1,0:T(8,128)(2,1)S(1)} %get-tuple-element.9.pick_ref, bf16[64,2048]{1,0:T(8,128)(2,1)S(1)} %get-tuple-element.10.kv_ref, ...), custom_call_target="tpu_custom_call" | custom-call | tf_op jit(solution)/shard_map/text/pallas_call | solution.py:373

commit v5 on v4

--- a/solution.py
+++ b/solution.py
@@ -252,9 +252,8 @@
         copy.wait()
     project(here, 0, half)
     key_swap.start()
-    project(here, half, 2 * half)
     swap(vis_ref, there, 0).wait_recv()
-    project(there, half, 2 * half)
+    project(pl.ds(0, keys), half, 2 * half)
     all_of(slots.at[: n - 1], send_sem).wait()
     vis_swap.wait_send()
     key_swap.wait_send()
@@ -340,15 +339,18 @@
                 expd = jnp.exp2((part - jnp.max(part, axis=0, keepdims=True)) * scale)
                 halves.append(expd * (1.0 / jnp.sum(expd, axis=0, keepdims=True)))
             probs.append(jnp.concatenate(halves, axis=0).astype(jnp.bfloat16))
-        out = lax.dot_general(
-            jnp.concatenate(probs, axis=1), v_two, (((0,), (0,)), ((), ())),
-            preferred_element_type=jnp.float32,
-        ).astype(jnp.bfloat16)
-        tokens = out.shape[0] // pairs
-        for j in range(pairs):
-            o_ref[:, g * span + j * wide : g * span + (j + 1) * wide] = out[
-                j * tokens : (j + 1) * tokens
-            ]
+        parts = [probs] if g < KVH - 1 else [[prob] for prob in probs]
+        j = 0
+        for part in parts:
+            out = lax.dot_general(
+                jnp.concatenate(part, axis=1), v_two, (((0,), (0,)), ((), ())),
+                preferred_element_type=jnp.float32,
+            ).astype(jnp.bfloat16)
+            tokens = out.shape[0] // len(part)
+            for i in range(len(part)):
+                at = g * span + j * wide
+                o_ref[:, at : at + wide] = out[i * tokens : (i + 1) * tokens]
+                j += 1
         cols = pl.ds(g * span, span)
         pltpu.make_async_copy(o_ref.at[:, cols], out_hbm.at[:, cols], out_sem).start()
 

time: 14.1 us -> 14 us (level)
  no operation moved by 1% of the time
where the time goes in v5:
time: 14 us; the launch traced here: 13.9 us
  Pallas kernels  12.6 us (90%)
  between operations  1.29 us (9%)
    pallas_call x1, Pallas kernels, gather_part(): pl.pallas_call(functools.partial(gather_kernel, n, images, rows, width, t...  10.7 us
    pallas_call x1, Pallas kernels, text_part(): pl.pallas_call(text_kernel, out_shape=(jax.ShapeDtypeStruct(shape, jnp.bf...  1.91 us

profile of v5, /device:TPU:0, one launch (start us, length us, event | category | flops | bytes accessed | tf_op | source)
XLA Modules:
  0.0 13.9 jit_solution(17788776475839307412)
XLA Ops:
  1.3 10.7 %vision.1 = (bf16[64,1280]{1,0:T(8,128)(2,1)S(1)}, f32[128,128]{1,0:T(8,128)S(1)}, bf16[16,64]{1,0:T(8,128)(2,1)S(1)}, bf16[64,2048]{1,0:T(8,128)(2,1)S(1)}, bf16[128,6144]{1,0:T(8,128)(2,1)S(1)}) custom-call(f32[1]{0:T(128)S(6)} %copy.11.gate_in, s32[2]{0:T(128)} %count_in.1, s32[1,128]{1,0:T(1,128)} %bitcast.1, bf16[2,4,1280]{2,1,0:T(4,128)(2,1)} %q_in.1, ...), custom_call_target="tpu_custom_call" | custom-call | tf_op jit(solution)/shard_map/vision/pallas_call | solution.py:274
  12.0 1.9 %text.1 = (bf16[2,4,1280]{2,1,0:T(4,128)(2,1)}, bf16[128,6144]{1,0:T(8,128)(2,1)}) custom-call(bf16[64,1280]{1,0:T(8,128)(2,1)S(1)} %get-tuple-element.7.vis_ref, f32[128,128]{1,0:T(8,128)S(1)} %get-tuple-element.8.bias_ref, bf16[16,64]{1,0:T(8,128)(2,1)S(1)} %get-tuple-element.9.pick_ref, bf16[64,2048]{1,0:T(8,128)(2,1)S(1)} %get-tuple-element.10.kv_ref, ...), custom_call_target="tpu_custom_call" | custom-call | tf_op jit(solution)/shard_map/text/pallas_call | solution.py:375

commit v6 on v5

--- a/solution.py
+++ b/solution.py
@@ -351,20 +351,20 @@
                 at = g * span + j * wide
                 o_ref[:, at : at + wide] = out[i * tokens : (i + 1) * tokens]
                 j += 1
-        cols = pl.ds(g * span, span)
-        pltpu.make_async_copy(o_ref.at[:, cols], out_hbm.at[:, cols], out_sem).start()
-
+            cols = pl.ds(g * span + (j - len(part)) * wide, len(part) * wide)
+            pltpu.make_async_copy(o_ref.at[:, cols], out_hbm.at[:, cols], out_sem).start()
+
+    for g in range(KVH):
+        attend(
+            g,
+            double(kv_ref[:, g * HD : (g + 1) * HD]),
+            double(kv_ref[:, half + g * HD : half + (g + 1) * HD]),
+        )
     local = jnp.dot(pick_ref[...], vis_ref[...], preferred_element_type=jnp.float32)
     for b in range(images):
         local_ref[b] = local[8 * b : 8 * b + rows].astype(jnp.bfloat16)
     local_copy = pltpu.make_async_copy(local_ref, vis_out, local_sem)
     local_copy.start()
-    for g in range(KVH):
-        attend(
-            g,
-            double(kv_ref[:, g * HD : (g + 1) * HD]),
-            double(kv_ref[:, half + g * HD : half + (g + 1) * HD]),
-        )
     local_copy.wait()
     pltpu.make_async_copy(o_ref, out_hbm, out_sem).wait()
 

time: 14 us -> 14 us (level)
  no operation moved by 1% of the time
where the time goes in v6:
time: 14 us; the launch traced here: 13.8 us
  Pallas kernels  12.6 us (90%)
  between operations  1.29 us (9%)
    pallas_call x1, Pallas kernels, gather_part(): pl.pallas_call(functools.partial(gather_kernel, n, images, rows, width, t...  10.7 us
    pallas_call x1, Pallas kernels, text_part(): pl.pallas_call(text_kernel, out_shape=(jax.ShapeDtypeStruct(shape, jnp.bf...  1.88 us

profile of v6, /device:TPU:0, one launch (start us, length us, event | category | flops | bytes accessed | tf_op | source)
XLA Modules:
  0.0 13.8 jit_solution(13451812866118348581)
XLA Ops:
  1.3 10.7 %vision.1 = (bf16[64,1280]{1,0:T(8,128)(2,1)S(1)}, f32[128,128]{1,0:T(8,128)S(1)}, bf16[16,64]{1,0:T(8,128)(2,1)S(1)}, bf16[64,2048]{1,0:T(8,128)(2,1)S(1)}, bf16[128,6144]{1,0:T(8,128)(2,1)S(1)}) custom-call(f32[1]{0:T(128)S(6)} %copy.11.gate_in, s32[2]{0:T(128)} %count_in.1, s32[1,128]{1,0:T(1,128)} %bitcast.1, bf16[2,4,1280]{2,1,0:T(4,128)(2,1)} %q_in.1, ...), custom_call_target="tpu_custom_call" | custom-call | tf_op jit(solution)/shard_map/vision/pallas_call | solution.py:274
  12.0 1.9 %text.1 = (bf16[2,4,1280]{2,1,0:T(4,128)(2,1)}, bf16[128,6144]{1,0:T(8,128)(2,1)}) custom-call(bf16[64,1280]{1,0:T(8,128)(2,1)S(1)} %get-tuple-element.7.vis_ref, f32[128,128]{1,0:T(8,128)S(1)} %get-tuple-element.8.bias_ref, bf16[16,64]{1,0:T(8,128)(2,1)S(1)} %get-tuple-element.9.pick_ref, bf16[64,2048]{1,0:T(8,128)(2,1)S(1)} %get-tuple-element.10.kv_ref, ...), custom_call_target="tpu_custom_call" | custom-call | tf_op jit(solution)/shard_map/text/pallas_call | solution.py:375

commit v7 on v6

--- a/solution.py
+++ b/solution.py
@@ -90,7 +90,7 @@
     gate_in, count_in, seen_in, q_in, k_in, v_in, r_in, w_in, text_in,
     vis_ref, bias_ref, pick_ref, kv_ref, text_ref,
     w_ref, other, slots, seen_ref, gate_ref, count_ref,
-    load_sem, small_sem, big_sem, send_sem, recv_sem, swap_sem,
+    load_sem, small_sem, send_sem, recv_sem, swap_sem,
 ):
     me = lax.axis_index("seq")
     chip, core = me // CORES, me % CORES
@@ -126,8 +126,8 @@
         pltpu.make_async_copy(seen_in, seen_ref, small_sem.at[2]),
     ]
     big = [
-        pltpu.make_async_copy(w_in, w_ref, big_sem.at[0]),
-        pltpu.make_async_copy(text_in, text_ref, big_sem.at[1]),
+        pltpu.make_async_copy(w_in, w_ref, small_sem.at[1]),
+        pltpu.make_async_copy(text_in, text_ref, small_sem.at[2]),
     ]
     for copy in small:
         copy.start()
@@ -151,11 +151,11 @@
             send(mine, part, there * CORES + core)
             send(other, part, there * CORES + 1 - core)
         send(other, part, partner)
+    for copy in small:
+        copy.wait()
     for copy in big:
         copy.start()
 
-    for copy in small:
-        copy.wait()
     place = lax.broadcasted_iota(jnp.int32, (length, tokens), 0)
     for b in range(images):
         ok = (place // (length // TILES) < count_ref[b]) & (seen_ref[...] >= b)
@@ -227,12 +227,12 @@
     there = pl.ds(pl.multiple_of((1 - core) * length, length), length)
     half = KVH * HD
 
-    def swap(ref, at, number):
+    def swap(ref, at, sent, number):
         return pltpu.make_async_remote_copy(
             src_ref=ref.at[at],
             dst_ref=ref.at[at],
-            send_sem=swap_sem.at[number],
-            recv_sem=swap_sem.at[number + 1],
+            send_sem=sent,
+            recv_sem=swap_sem.at[number],
             device_id={"seq": partner},
             device_id_type=MESH,
         )
@@ -245,19 +245,19 @@
                 vis, w_ref[:, cols], preferred_element_type=jnp.float32
             ).astype(jnp.bfloat16)
 
-    vis_swap = swap(vis_ref, here, 0)
-    key_swap = swap(kv_ref, (here, pl.ds(0, half)), 2)
+    vis_swap = swap(vis_ref, here, load_sem, 0)
+    key_swap = swap(kv_ref, (here, pl.ds(0, half)), small_sem.at[0], 1)
     vis_swap.start()
     for copy in big:
         copy.wait()
     project(here, 0, half)
     key_swap.start()
-    swap(vis_ref, there, 0).wait_recv()
+    swap(vis_ref, there, load_sem, 0).wait_recv()
     project(pl.ds(0, keys), half, 2 * half)
     all_of(slots.at[: n - 1], send_sem).wait()
     vis_swap.wait_send()
     key_swap.wait_send()
-    swap(kv_ref, (there, pl.ds(0, half)), 2).wait_recv()
+    swap(kv_ref, (there, pl.ds(0, half)), small_sem.at[0], 1).wait_recv()
 
 
 def gather_part(n, q, k, v, r, gate, count, seen, w_kv, text):
@@ -291,10 +291,9 @@
             pltpu.SMEM((images,), jnp.int32),
             pltpu.SemaphoreType.DMA,
             pltpu.SemaphoreType.DMA((3,)),
-            pltpu.SemaphoreType.DMA((2,)),
             pltpu.SemaphoreType.DMA,
             pltpu.SemaphoreType.DMA((2,)),
-            pltpu.SemaphoreType.DMA((4,)),
+            pltpu.SemaphoreType.DMA((2,)),
         ],
         compiler_params=pltpu.CompilerParams(
             collective_id=0, has_side_effects=True, vmem_limit_bytes=GRANT

time: 14 us -> 14 us (level)
  no operation moved by 1% of the time
where the time goes in v7:
time: 14 us; the launch traced here: 13.8 us
  Pallas kernels  12.5 us (89%)
  between operations  1.29 us (9%)
    pallas_call x1, Pallas kernels, gather_part(): pl.pallas_call(functools.partial(gather_kernel, n, images, rows, width, t...  10.6 us
    pallas_call x1, Pallas kernels, text_part(): pl.pallas_call(text_kernel, out_shape=(jax.ShapeDtypeStruct(shape, jnp.bf...  1.88 us

profile of v7, /device:TPU:0, one launch (start us, length us, event | category | flops | bytes accessed | tf_op | source)
XLA Modules:
  0.0 13.8 jit_solution(9689326938048163110)
XLA Ops:
  1.3 10.6 %vision.1 = (bf16[64,1280]{1,0:T(8,128)(2,1)S(1)}, f32[128,128]{1,0:T(8,128)S(1)}, bf16[16,64]{1,0:T(8,128)(2,1)S(1)}, bf16[64,2048]{1,0:T(8,128)(2,1)S(1)}, bf16[128,6144]{1,0:T(8,128)(2,1)S(1)}) custom-call(f32[1]{0:T(128)S(6)} %copy.11.gate_in, s32[2]{0:T(128)} %count_in.1, s32[1,128]{1,0:T(1,128)} %bitcast.1, bf16[2,4,1280]{2,1,0:T(4,128)(2,1)} %q_in.1, ...), custom_call_target="tpu_custom_call" | custom-call | tf_op jit(solution)/shard_map/vision/pallas_call | solution.py:274
  11.9 1.9 %text.1 = (bf16[2,4,1280]{2,1,0:T(4,128)(2,1)}, bf16[128,6144]{1,0:T(8,128)(2,1)}) custom-call(bf16[64,1280]{1,0:T(8,128)(2,1)S(1)} %get-tuple-element.7.vis_ref, f32[128,128]{1,0:T(8,128)S(1)} %get-tuple-element.8.bias_ref, bf16[16,64]{1,0:T(8,128)(2,1)S(1)} %get-tuple-element.9.pick_ref, bf16[64,2048]{1,0:T(8,128)(2,1)S(1)} %get-tuple-element.10.kv_ref, ...), custom_call_target="tpu_custom_call" | custom-call | tf_op jit(solution)/shard_map/text/pallas_call | solution.py:374

commit v8 on v7

--- a/solution.py
+++ b/solution.py
@@ -90,7 +90,7 @@
     gate_in, count_in, seen_in, q_in, k_in, v_in, r_in, w_in, text_in,
     vis_ref, bias_ref, pick_ref, kv_ref, text_ref,
     w_ref, other, slots, seen_ref, gate_ref, count_ref,
-    load_sem, small_sem, send_sem, recv_sem, swap_sem,
+    load_sem, small_sem, recv_sem, swap_sem,
 ):
     me = lax.axis_index("seq")
     chip, core = me // CORES, me % CORES
@@ -133,6 +133,8 @@
         copy.start()
     pl.semaphore_wait(barrier, len(others))
     all_of(slots.at[:2], load_sem).wait()
+    for copy in small:
+        copy.wait()
 
     cuts = (pl.ds(0, 3), pl.ds(3, 1))
 
@@ -140,7 +142,7 @@
         pltpu.make_async_remote_copy(
             src_ref=src.at[cuts[part]],
             dst_ref=slots.at[me, cuts[part]],
-            send_sem=send_sem,
+            send_sem=small_sem.at[0],
             recv_sem=recv_sem.at[part],
             device_id={"seq": dev},
             device_id_type=MESH,
@@ -151,8 +153,6 @@
             send(mine, part, there * CORES + core)
             send(other, part, there * CORES + 1 - core)
         send(other, part, partner)
-    for copy in small:
-        copy.wait()
     for copy in big:
         copy.start()
 
@@ -246,7 +246,7 @@
             ).astype(jnp.bfloat16)
 
     vis_swap = swap(vis_ref, here, load_sem, 0)
-    key_swap = swap(kv_ref, (here, pl.ds(0, half)), small_sem.at[0], 1)
+    key_swap = swap(kv_ref, (here, pl.ds(0, half)), small_sem.at[1], 1)
     vis_swap.start()
     for copy in big:
         copy.wait()
@@ -254,10 +254,10 @@
     key_swap.start()
     swap(vis_ref, there, load_sem, 0).wait_recv()
     project(pl.ds(0, keys), half, 2 * half)
-    all_of(slots.at[: n - 1], send_sem).wait()
+    all_of(slots.at[: n - 1], small_sem.at[0]).wait()
     vis_swap.wait_send()
     key_swap.wait_send()
-    swap(kv_ref, (there, pl.ds(0, half)), small_sem.at[0], 1).wait_recv()
+    swap(kv_ref, (there, pl.ds(0, half)), small_sem.at[1], 1).wait_recv()
 
 
 def gather_part(n, q, k, v, r, gate, count, seen, w_kv, text):
@@ -291,7 +291,6 @@
             pltpu.SMEM((images,), jnp.int32),
             pltpu.SemaphoreType.DMA,
             pltpu.SemaphoreType.DMA((3,)),
-            pltpu.SemaphoreType.DMA,
             pltpu.SemaphoreType.DMA((2,)),
             pltpu.SemaphoreType.DMA((2,)),
         ],

time: 14 us -> 14 us (level)
  no operation moved by 1% of the time
where the time goes in v8:
time: 14 us; the launch traced here: 13.8 us
  Pallas kernels  12.5 us (89%)
  between operations  1.29 us (9%)
    pallas_call x1, Pallas kernels, gather_part(): pl.pallas_call(functools.partial(gather_kernel, n, images, rows, width, t...  10.7 us
    pallas_call x1, Pallas kernels, text_part(): pl.pallas_call(text_kernel, out_shape=(jax.ShapeDtypeStruct(shape, jnp.bf...  1.88 us

profile of v8, /device:TPU:0, one launch (start us, length us, event | category | flops | bytes accessed | tf_op | source)
XLA Modules:
  0.0 13.8 jit_solution(14612552691412189353)
XLA Ops:
  1.3 10.7 %vision.1 = (bf16[64,1280]{1,0:T(8,128)(2,1)S(1)}, f32[128,128]{1,0:T(8,128)S(1)}, bf16[16,64]{1,0:T(8,128)(2,1)S(1)}, bf16[64,2048]{1,0:T(8,128)(2,1)S(1)}, bf16[128,6144]{1,0:T(8,128)(2,1)S(1)}) custom-call(f32[1]{0:T(128)S(6)} %copy.11.gate_in, s32[2]{0:T(128)} %count_in.1, s32[1,128]{1,0:T(1,128)} %bitcast.1, bf16[2,4,1280]{2,1,0:T(4,128)(2,1)} %q_in.1, ...), custom_call_target="tpu_custom_call" | custom-call | tf_op jit(solution)/shard_map/vision/pallas_call | solution.py:274
  11.9 1.9 %text.1 = (bf16[2,4,1280]{2,1,0:T(4,128)(2,1)}, bf16[128,6144]{1,0:T(8,128)(2,1)}) custom-call(bf16[64,1280]{1,0:T(8,128)(2,1)S(1)} %get-tuple-element.7.vis_ref, f32[128,128]{1,0:T(8,128)S(1)} %get-tuple-element.8.bias_ref, bf16[16,64]{1,0:T(8,128)(2,1)S(1)} %get-tuple-element.9.pick_ref, bf16[64,2048]{1,0:T(8,128)(2,1)S(1)} %get-tuple-element.10.kv_ref, ...), custom_call_target="tpu_custom_call" | custom-call | tf_op jit(solution)/shard_map/text/pallas_call | solution.py:373
